TPU v7x, 32 devices: a whole 2x2x4 slice. The times are simulated.
32 devices in a mesh: node: 8 (over z, x), mp: 4 (over y, core).
Axes of the slice: x: 2, y: 2, z: 4, core: 2. Of those that a mesh axis runs over, the one named last changes fastest.
Arguments:
- queries: bfloat16 [32, 64, 128], P('node', 'mp'), may hold values from -8 to 8
- root_keys: bfloat16 [16384, 8, 128], P('node', 'mp'), may hold values from -6 to 6
- root_values: bfloat16 [16384, 8, 128], P('node', 'mp'), may hold values from -6 to 6
- mid_keys: bfloat16 [8, 1024, 8, 128], P('node', None, 'mp'), may hold values from -6 to 6
- mid_values: bfloat16 [8, 1024, 8, 128], P('node', None, 'mp'), may hold values from -6 to 6
- leaf_keys: bfloat16 [32, 256, 8, 128], P('node', None, 'mp'), may hold values from -6 to 6
- leaf_values: bfloat16 [32, 256, 8, 128], P('node', None, 'mp'), may hold values from -6 to 6
- mid_length: int32 [8], replicated, may hold values from 1 to 1024
- leaf_length: int32 [32], P('node'), may hold values from 1 to 256
- branch_mid: int32 [32, 1], replicated, may hold values from 0 to 7; in each aligned block of 32 rows (0 to 31, 32 to 63, ...) at most 8 rows name the same one
- residual: bfloat16 [32, 8192], P(None, 'node'), may hold values from -6 to 6
- norm_gain: float32 [8192], P('node'), may hold values from 0.5 to 1.5
- out_weight: bfloat16 [8192, 8192], P('mp', 'node'), may hold values from -0.0625 to 0.0625
- gate_weight: bfloat16 [8192, 28672], P('node', 'mp'), may hold values from -0.0625 to 0.0625
- up_weight: bfloat16 [8192, 28672], P('node', 'mp'), may hold values from -0.0625 to 0.0625
- down_weight: bfloat16 [28672, 8192], P('mp', 'node'), may hold values from -0.03125 to 0.03125
Outputs:
- layer_out: bfloat16 [32, 8192], P('mp', 'node')
Inputs may be any that keep to these rules, and one draw needn't show every extreme that they name: `branch_mid`: every inner tree node lies on the path of 1 to 8 branches, and some node on exactly 8.
All inputs are finite; a program needn't handle non-finite values.
Results may differ from a plain program's by a relative error of at most 0.015.
Values may be sent and summed in bfloat16 or wider, within the bound.
A program may use at most 128 MiB of HBM per device.

v0:
```python
import jax
import jax.numpy as jnp
from jax import lax
from jax.sharding import PartitionSpec as P

D = 8192
CAP = 8
masked_score = -1e30
norm_eps = 1e-05


def partial_scores(grouped, key_block, value_block, usable, scaling):
    scores = (
        jnp.einsum("bkgd,lkd->bkgl", grouped, key_block, preferred_element_type=jnp.float32)
        * scaling
    )
    masking = usable[:, None, None, :]
    scores = jnp.where(masking, scores, masked_score)
    highest = jnp.max(scores, axis=-1)
    weights = jnp.where(masking, jnp.exp(scores - highest[..., None]), 0.0)
    weighted = jnp.einsum(
        "bkgl,lkd->bkgd",
        weights.astype(jnp.bfloat16),
        value_block,
        preferred_element_type=jnp.float32,
    )
    return (highest, jnp.sum(weights, axis=-1), weighted)


def combine_parts(earlier, later):
    highest = jnp.maximum(earlier[0], later[0])
    first_factor = jnp.exp(earlier[0] - highest)
    second_factor = jnp.exp(later[0] - highest)
    totals = earlier[1] * first_factor + later[1] * second_factor
    weighted = earlier[2] * first_factor[..., None] + later[2] * second_factor[..., None]
    return (highest, totals, weighted)


def on_device(
    queries,
    root_keys,
    root_values,
    mid_keys,
    mid_values,
    leaf_keys,
    leaf_values,
    mid_length,
    leaf_length,
    branch_mid,
    residual,
    norm_gain,
    out_weight,
    gate_weight,
    up_weight,
    down_weight,
):
    owned = queries.shape[0]
    local_heads = queries.shape[1]
    head_size = queries.shape[2]
    local_groups = root_keys.shape[1]
    group_size = local_heads // local_groups
    scaling = head_size ** (-0.5)
    node_count = lax.axis_size("node")
    gathered = lax.all_gather(queries, "node", axis=0, tiled=True)
    every_branch = gathered.shape[0]
    grouped = gathered.reshape(every_branch, local_groups, group_size, head_size)
    root_usable = jnp.ones((every_branch, root_keys.shape[0]), dtype=bool)
    root_part = partial_scores(grouped, root_keys, root_values, root_usable, scaling)
    local_mids = mid_keys.shape[0]
    node_ids = lax.axis_index("node") * local_mids + jnp.arange(local_mids, dtype=jnp.int32)
    routing = branch_mid[:, 0]
    matching = routing[None, :] == node_ids[:, None]
    ranking = jnp.cumsum(matching.astype(jnp.int32), axis=1) - 1
    selected = matching[:, None, :] & (
        ranking[:, None, :] == jnp.arange(CAP, dtype=jnp.int32)[None, :, None]
    )
    picked = jnp.einsum(
        "ncb,bkgd->nckgd",
        selected.astype(jnp.bfloat16),
        grouped,
        preferred_element_type=jnp.float32,
    ).astype(jnp.bfloat16)
    slot_index = jnp.arange(mid_keys.shape[1])

    def node_partial(inputs):
        node_queries, node_keys, node_values, node_id = inputs
        usable = jnp.broadcast_to(
            slot_index[None, :] < mid_length[node_id], (CAP, slot_index.shape[0])
        )
        return partial_scores(node_queries, node_keys, node_values, usable, scaling)

    node_high, node_totals, node_weighted = lax.map(
        node_partial, (picked, mid_keys, mid_values, node_ids)
    )
    chosen = selected.astype(jnp.float32)
    covered = jnp.sum(chosen, axis=(0, 1))
    back_high = (
        jnp.einsum("ncb,nckg->bkg", chosen, node_high, precision=lax.Precision.HIGHEST)
        + ((1.0 - covered) * masked_score)[:, None, None]
    )
    back_totals = jnp.einsum("ncb,nckg->bkg", chosen, node_totals, precision=lax.Precision.HIGHEST)
    back_weighted = jnp.einsum(
        "ncb,nckgd->bkgd", chosen, node_weighted, precision=lax.Precision.HIGHEST
    )
    shared_part = combine_parts(root_part, (back_high, back_totals, back_weighted))
    peaks, totals, weighted = (
        lax.all_to_all(shared_part[0], "node", split_axis=0, concat_axis=0, tiled=True),
        lax.all_to_all(shared_part[1], "node", split_axis=0, concat_axis=0, tiled=True),
        lax.all_to_all(shared_part[2], "node", split_axis=0, concat_axis=0, tiled=True),
    )
    peaks = peaks.reshape(node_count, owned, local_groups, group_size)
    totals = totals.reshape(node_count, owned, local_groups, group_size)
    weighted = weighted.reshape(node_count, owned, local_groups, group_size, head_size)
    highest = jnp.max(peaks, axis=0)
    factor = jnp.exp(peaks - highest[None])
    merged = (
        highest,
        jnp.sum(totals * factor, axis=0),
        jnp.sum(weighted * factor[..., None], axis=0),
    )
    own_grouped = queries.reshape(owned, local_groups, group_size, head_size)
    leaf_scores = (
        jnp.einsum("bkgd,blkd->bkgl", own_grouped, leaf_keys, preferred_element_type=jnp.float32)
        * scaling
    )
    leaf_usable = (jnp.arange(leaf_keys.shape[1])[None, :] < leaf_length[:, None])[:, None, None, :]
    leaf_scores = jnp.where(leaf_usable, leaf_scores, masked_score)
    leaf_peak = jnp.max(leaf_scores, axis=-1)
    leaf_weights = jnp.where(leaf_usable, jnp.exp(leaf_scores - leaf_peak[..., None]), 0.0)
    leaf_weighted = jnp.einsum(
        "bkgl,blkd->bkgd",
        leaf_weights.astype(jnp.bfloat16),
        leaf_values,
        preferred_element_type=jnp.float32,
    )
    final_part = combine_parts(merged, (leaf_peak, jnp.sum(leaf_weights, axis=-1), leaf_weighted))
    attended = (
        (final_part[2] / final_part[1][..., None])
        .reshape(owned, local_heads * head_size)
        .astype(jnp.bfloat16)
    )
    projected = jnp.dot(
        lax.all_gather(attended, "node", axis=0, tiled=True),
        out_weight,
        preferred_element_type=jnp.float32,
    )
    projected = lax.psum(projected.astype(jnp.bfloat16), "mp").astype(jnp.float32)
    stream = residual.astype(jnp.float32) + projected
    squares = lax.psum(jnp.sum(stream * stream, axis=1), "node")
    normed = (stream * lax.rsqrt(squares[:, None] / D + norm_eps) * norm_gain[None, :]).astype(
        jnp.bfloat16
    )
    out_rows = every_branch // lax.axis_size("mp")
    gate, upward = (
        lax.psum(
            jnp.dot(normed, gate_weight, preferred_element_type=jnp.float32).astype(jnp.bfloat16),
            "node",
        ).astype(jnp.float32),
        lax.psum(
            jnp.dot(normed, up_weight, preferred_element_type=jnp.float32).astype(jnp.bfloat16),
            "node",
        ).astype(jnp.float32),
    )
    act = (jax.nn.silu(gate) * upward).astype(jnp.bfloat16)
    mlp_rows = lax.psum_scatter(
        jnp.dot(act, down_weight, preferred_element_type=jnp.float32).astype(jnp.bfloat16),
        "mp",
        scatter_dimension=0,
        tiled=True,
    ).astype(jnp.float32)
    stream_rows = lax.dynamic_slice_in_dim(stream, lax.axis_index("mp") * out_rows, out_rows, 0)
    return (stream_rows + mlp_rows).astype(jnp.bfloat16)


def solution(mesh):
    in_specs = (
        P("node", "mp", None),
        P("node", "mp", None),
        P("node", "mp", None),
        P("node", None, "mp", None),
        P("node", None, "mp", None),
        P("node", None, "mp", None),
        P("node", None, "mp", None),
        P(),
        P("node"),
        P(),
        P(None, "node"),
        P("node"),
        P("mp", "node"),
        P("node", "mp"),
        P("node", "mp"),
        P("mp", "node"),
    )
    out_specs = P("mp", "node")
    return jax.shard_map(
        on_device, mesh=mesh, in_specs=in_specs, out_specs=out_specs, check_vma=False
    )
```

profile of v0, /device:TPU:0, one launch (start us, length us, event | category | flops | bytes accessed | tf_op | source)
XLA Modules:
  0.0 297.3 jit_solution(1106771095615868161)
XLA Ops:
  6.5 0.0 copy-start
  6.5 1.3 dynamic_slice.18
  7.9 0.6 iota_compare_fusion.2
  8.5 0.7 compare_bitcast_fusion
  9.2 0.1 copy.97
  9.3 0.1 reduce-window.7
  9.3 0.1 add_reduce_fusion
  9.5 32.5 %all_gather.6 = bf16[32,16,128]{2,1,0:T(8,128)(2,1)S(1)} all-gather(bf16[4,16,128]{2,1,0:T(8,128)(2,1)} %param.16), channel_id=1, replica_groups=mesh['node'=8,'mp'=4] {'node'}, dimensions={0}, use_global_device_ids=true | all-gather | bytes 147456 | tf_op jit(solution)/shard_map/all_gather | solution.py:64
  42.1 0.1 convolution_convert_fusion.4
  42.2 1.4 fusion.79
  43.6 0.1 copy.100
  43.7 0.2 fusion.37
  43.9 0.1 copy.114
  44.0 0.0 copy-start.7
  44.0 2.1 bitcast_reduce_fusion
  46.1 0.0 copy-start.1
  46.1 0.1 subtract_exponential_fusion.1
  46.2 1.8 copy-done.1
  48.0 0.8 fusion.1
  48.9 0.1 fusion.22
  49.0 0.7 copy.115
  49.7 5.5 %all-to-all-start.2 = ((f32[32,2,8]{2,1,0:T(2,128)}), f32[32,2,8]{2,1,0:T(2,128)S(1)}, u32[]{:S(2)}, u32[]{:S(2)}) async-start(f32[32,2,8]{2,1,0:T(2,128)} %copy.115), calls=%async_computation.2 | async-start | bytes 65536 | tf_op jit(solution)/shard_map/all_to_all | solution.py:108
  55.1 0.0 copy-done.9
  55.1 0.1 iota_compare_fusion
  55.2 0.0 copy-done.7
  55.2 0.3 convolution_bitcast_fusion
  55.5 0.0 copy-done
  55.5 0.0 copy-start.8
  55.5 3.3 %fusion.13 = f32[32,2,8,128]{3,0,2,1:T(8,128)S(1)} fusion(f32[2,2048,32,8]{1,2,3,0:T(8,128)} %copy-done.1, f32[32,2,8]{0,2,1:T(8,128)S(1)} %get-tuple-element.48, bf16[2048,2,128,1]{2,1,0,3:T(2,128)(2,1)S(1)} %bitcast.75, f32[32,2,8]{0,2,1:T(8,128)S(1)} %subtract_exponential_fusion.2), kind=kOutput, calls=%fused_computation.16 | convolution fusion | flops 271646720 | bytes 5509120 | tf_op jit(solution)/shard_map/bkgl,lkd->bkgd/dot_general | solution.py:21
  58.8 0.0 copy-done.4
  58.8 0.0 copy-done.6
  58.8 0.3 fusion.80
  59.2 0.7 copy.104
  59.9 2.0 all-to-all-done.2
  61.8 4.2 %all-to-all-start.1 = ((f32[32,2,8]{2,1,0:T(2,128)}), f32[32,2,8]{2,1,0:T(2,128)S(1)}, u32[]{:S(2)}, u32[]{:S(2)}) async-start(f32[32,2,8]{2,1,0:T(2,128)} %copy.104), calls=%async_computation.1 | async-start | bytes 65536 | tf_op jit(solution)/shard_map/all_to_all | solution.py:107
  66.0 0.3 fusion.12
  66.3 0.8 copy.103
  67.2 5.5 %all-to-all-done.1 = f32[32,2,8]{2,1,0:T(2,128)S(1)} async-done(((f32[32,2,8]{2,1,0:T(2,128)}), f32[32,2,8]{2,1,0:T(2,128)S(1)}, u32[]{:S(2)}, u32[]{:S(2)}) %all-to-all-start.1) | async-done | bytes 2080 | tf_op jit(solution)/shard_map/all_to_all | solution.py:107
  72.7 3.4 %all-to-all-start = ((f32[32,2,8,128]{3,2,1,0:T(8,128)}), f32[32,2,8,128]{3,2,1,0:T(8,128)S(1)}, u32[]{:S(2)}, u32[]{:S(2)}) async-start(f32[32,2,8,128]{3,2,1,0:T(8,128)} %copy.103), calls=%async_computation | async-start | bytes 524288 | tf_op jit(solution)/shard_map/all_to_all | solution.py:109
  76.1 0.0 all-reduce.4.cloned.1.call-start
  76.1 0.2 fusion.45
  76.5 7.9 %all-to-all-done = f32[32,2,8,128]{3,2,1,0:T(8,128)S(1)} async-done(((f32[32,2,8,128]{3,2,1,0:T(8,128)}), f32[32,2,8,128]{3,2,1,0:T(8,128)S(1)}, u32[]{:S(2)}, u32[]{:S(2)}) %all-to-all-start) | async-done | bytes 262176 | tf_op jit(solution)/shard_map/all_to_all | solution.py:109
  84.3 0.1 fusion.40
  84.5 0.0 copy-done.8
  84.5 0.2 fusion.19
  84.8 30.6 %all-gather = bf16[8,4,2048]{2,1,0:T(4,128)(2,1)S(1)} all-gather(bf16[1,4,2048]{2,1,0:T(4,128)(2,1)S(1)} %reshape.273), channel_id=1, replica_groups=mesh['node'=8,'mp'=4] {'node'}, dimensions={0}, use_global_device_ids=true | all-gather | bytes 147456 | tf_op jit(solution)/shard_map/all_gather | solution.py:143
  115.4 3.6 %convolution_convert_fusion.3 = bf16[32,1024]{1,0:T(8,128)(2,1)} fusion(bf16[32,2048]{1,0:T(8,128)(2,1)S(1)} %reshape.274, bf16[2048,1024]{1,0:T(8,128)(2,1)} %param.28), kind=kOutput, calls=%fused_computation.20 | convolution fusion | flops 134250496 | bytes 4390912 | tf_op jit(solution)/shard_map/dot_general | solution.py:142
  119.0 0.0 all-reduce.4.cloned.1.call-update
  119.0 0.0 all-reduce.6.cloned.1.call-start
  119.1 30.0 %all-reduce.4.cloned.1.call-done = bf16[32,1024]{1,0:T(8,128)(2,1)} async-done(((bf16[32,1024]{1,0:T(8,128)(2,1)}), bf16[32,1024]{1,0:T(8,128)(2,1)}) %all-reduce.4.cloned.1.call-update) | async-done | bytes 65552 | tf_op jit(solution)/shard_map/psum | solution.py:147
  149.1 0.0 copy-done.2
  149.1 1.0 convert_add_fusion
  150.1 21.4 %psum.29 = f32[32]{0:T(128)S(1)} all-reduce(f32[32]{0:T(128)S(1)} %get-tuple-element.45), channel_id=1, replica_groups=mesh['node'=8,'mp'=4] {'node'}, use_global_device_ids=true, to_apply=%region_13.14 | all-reduce | flops 32 | bytes 256 | tf_op jit(solution)/shard_map/psum | solution.py:149
  171.4 0.0 copy-done.5
  171.4 8.7 %convolution_convert_fusion = bf16[32,7168]{1,0:T(8,128)(2,1)} fusion(bf16[1024,7168]{1,0:T(8,128)(2,1)} %param.30, f32[1024]{0:T(1024)S(1)} %copy-done.5, f32[32]{0:T(128)S(1)} %add_rsqrt_fusion, bf16[32,1024]{1,0:T(8,128)(2,1)} %all-reduce.4.cloned.1.call-done, bf16[32,1024]{1,0:T(8,128)(2,1)S(1)} %copy-done.2), kind=kOutput, calls=%fused_computation | convolution fusion | flops 470188032 | bytes 15274112 | tf_op jit(solution)/shard_map/dot_general | solution.py:160
  180.1 0.0 copy-done.3
  180.1 8.6 %convolution_convert_fusion.1 = bf16[32,7168]{1,0:T(8,128)(2,1)} fusion(bf16[1024,7168]{1,0:T(8,128)(2,1)} %param.29, f32[1024]{0:T(1024)S(1)} %copy-done.5, f32[32]{0:T(128)S(1)} %add_rsqrt_fusion, bf16[32,1024]{1,0:T(8,128)(2,1)S(1)} %copy-done.3, bf16[32,1024]{1,0:T(8,128)(2,1)S(1)} %copy-done.2), kind=kOutput, calls=%fused_computation.1 | convolution fusion | flops 470188032 | bytes 15274112 | tf_op jit(solution)/shard_map/dot_general | solution.py:156
  188.7 0.0 all-reduce.6.cloned.1.call-update
  188.7 0.0 reduce-scatter.2.cloned.1.call-start
  188.8 73.1 %all-reduce.6.cloned.1.call-done = (bf16[32,7168]{1,0:T(8,128)(2,1)}, bf16[32,7168]{1,0:T(8,128)(2,1)}) async-done(((bf16[32,7168]{1,0:T(8,128)(2,1)}, bf16[32,7168]{1,0:T(8,128)(2,1)}), (bf16[32,7168]{1,0:T(8,128)(2,1)}, bf16[32,7168]{1,0:T(8,128)(2,1)})) %all-reduce.6.cloned.1.call-update) | async-done | bytes 917520 | tf_op jit(solution)/shard_map/psum | solution.py:159
  261.8 8.7 %convolution_convert_fusion.2 = bf16[32,1024]{1,0:T(8,128)(2,1)} fusion(bf16[7168,1024]{1,0:T(8,128)(2,1)} %param.31, bf16[32,7168]{1,0:T(8,128)(2,1)} %get-tuple-element.23, bf16[32,7168]{1,0:T(8,128)(2,1)} %get-tuple-element.24), kind=kOutput, calls=%fused_computation.19 | convolution fusion | flops 471629824 | bytes 15663104 | tf_op jit(solution)/shard_map/dot_general | solution.py:166
  270.6 0.0 reduce-scatter.2.cloned.1.call-update
  270.6 18.8 %reduce-scatter.2.cloned.1.call-done = bf16[8,1024]{1,0:T(8,128)(2,1)} async-done(((bf16[32,1024]{1,0:T(8,128)(2,1)}), bf16[8,1024]{1,0:T(8,128)(2,1)}) %reduce-scatter.2.cloned.1.call-update) | async-done | bytes 16400 | tf_op jit(solution)/shard_map/reduce_scatter | solution.py:165
  289.4 1.3 add_convert_fusion
  (21 shorter events, 0.2 us)
Async XLA Ops:
  6.5 49.0 %copy-start = (bf16[2048,2,128]{2,1,0:T(2,128)(2,1)S(1)}, bf16[2048,2,128]{2,1,0:T(2,128)(2,1)}, u32[]{:S(2)}) copy-start(bf16[2048,2,128]{2,1,0:T(2,128)(2,1)} %param.18) | copy-start | bytes 3145732
  44.0 11.1 %copy-start.9 = (s32[4]{0:T(128)S(1)}, s32[4]{0:T(128)}, u32[]{:S(2)}) copy-start(s32[4]{0:T(128)} %param.24) | copy-start | bytes 52
  44.0 11.2 %copy-start.7 = (bf16[1,1024,2,128]{3,2,1,0:T(2,128)(2,1)S(1)}, bf16[1,1024,2,128]{3,2,1,0:T(2,128)(2,1)}, u32[]{:S(2)}) copy-start(bf16[1,1024,2,128]{3,2,1,0:T(2,128)(2,1)} %param.20) | copy-start | bytes 1572868
  46.1 1.9 copy-start.1
  48.9 10.0 %copy-start.4 = (bf16[4,256,2,128]{3,2,1,0:T(2,128)(2,1)S(1)}, bf16[4,256,2,128]{3,2,1,0:T(2,128)(2,1)}, u32[]{:S(2)}) copy-start(bf16[4,256,2,128]{3,2,1,0:T(2,128)(2,1)} %param.21) | copy-start | bytes 1572868
  48.9 10.0 %copy-start.6 = (bf16[4,16,128]{2,1,0:T(8,128)(2,1)S(1)}, bf16[4,16,128]{2,1,0:T(8,128)(2,1)}, u32[]{:S(2)}) copy-start(bf16[4,16,128]{2,1,0:T(8,128)(2,1)} %param.16) | copy-start | bytes 49156
  49.7 12.1 %all-to-all-start.2 = ((f32[32,2,8]{2,1,0:T(2,128)}), f32[32,2,8]{2,1,0:T(2,128)S(1)}, u32[]{:S(2)}, u32[]{:S(2)}) async-start(f32[32,2,8]{2,1,0:T(2,128)} %copy.115), calls=%async_computation.2 | async-start | bytes 65536 | tf_op jit(solution)/shard_map/all_to_all | solution.py:108
  55.5 29.0 %copy-start.8 = (bf16[4,256,2,128]{3,2,1,0:T(2,128)(2,1)S(1)}, bf16[4,256,2,128]{3,2,1,0:T(2,128)(2,1)}, u32[]{:S(2)}) copy-start(bf16[4,256,2,128]{3,2,1,0:T(2,128)(2,1)} %param.22) | copy-start | bytes 1572868
  59.9 89.2 %copy-start.2 = (bf16[32,1024]{1,0:T(8,128)(2,1)S(1)}, bf16[32,1024]{1,0:T(8,128)(2,1)}, u32[]{:S(2)}) copy-start(bf16[32,1024]{1,0:T(8,128)(2,1)} %param.26) | copy-start | bytes 196612
  61.8 10.9 %all-to-all-start.1 = ((f32[32,2,8]{2,1,0:T(2,128)}), f32[32,2,8]{2,1,0:T(2,128)S(1)}, u32[]{:S(2)}, u32[]{:S(2)}) async-start(f32[32,2,8]{2,1,0:T(2,128)} %copy.104), calls=%async_computation.1 | async-start | bytes 65536 | tf_op jit(solution)/shard_map/all_to_all | solution.py:107
  66.0 105.4 %copy-start.5 = (f32[1024]{0:T(1024)S(1)}, f32[1024]{0:T(1024)}, u32[]{:S(2)}) copy-start(f32[1024]{0:T(1024)} %param.27) | copy-start | bytes 12292
  72.7 11.7 %all-to-all-start = ((f32[32,2,8,128]{3,2,1,0:T(8,128)}), f32[32,2,8,128]{3,2,1,0:T(8,128)S(1)}, u32[]{:S(2)}, u32[]{:S(2)}) async-start(f32[32,2,8,128]{3,2,1,0:T(8,128)} %copy.103), calls=%async_computation | async-start | bytes 524288 | tf_op jit(solution)/shard_map/all_to_all | solution.py:109
  76.1 73.0 %all-reduce.4.cloned.1.call-start = ((), (), s32[]{:S(2)}) async-start(), calls=%async_computation.4 | async-start | bytes 131072 | tf_op jit(solution)/shard_map/psum | solution.py:147
  119.0 142.8 %all-reduce.6.cloned.1.call-start = ((), (), s32[]{:S(2)}) async-start(), calls=%async_computation.6 | async-start | bytes 1835008 | tf_op jit(solution)/shard_map/psum | solution.py:159
  171.4 8.7 %copy-start.3 = (bf16[32,1024]{1,0:T(8,128)(2,1)S(1)}, bf16[32,1024]{1,0:T(8,128)(2,1)}, u32[]{:S(2)}) copy-start(bf16[32,1024]{1,0:T(8,128)(2,1)} %all-reduce.4.cloned.1.call-done) | copy-start | bytes 196612
  188.7 100.7 %reduce-scatter.2.cloned.1.call-start = ((), (), s32[]{:S(2)}) async-start(), calls=%async_computation.5 | async-start | bytes 81920 | tf_op jit(solution)/shard_map/reduce_scatter | solution.py:165
Sparse Core Ops, SparseCore 0:
  119.1 29.9 all-reduce.3
  188.9 72.9 all-reduce.5
  270.7 18.6 reduce-scatter.1
where the time goes:
time: 298 us; the launch traced here: 297 us
  waiting for transfers between devices  137 us (46%)
  blocking collectives  84.5 us (28%)
  matrix products  38 us (13%)
  between operations  13.3 us (4%)
  starting transfers between devices  13.1 us (4%)
  local copies, waits for them, and re-layouts  5.71 us (2%)
  other arithmetic  5.33 us (2%)
    psum x1, waiting for transfers between devices, on_device(): lax.psum(jnp.dot(normed, up_weight, preferred_element_type=jnp.float32).a...  73.1 us
    all_gather x1, blocking collectives, on_device(): gathered = lax.all_gather(queries, 'node', axis=0, tiled=True)  32.5 us
    all_gather x1, blocking collectives, on_device(): lax.all_gather(attended, 'node', axis=0, tiled=True)  30.6 us
    psum x1, waiting for transfers between devices, on_device(): lax.psum(projected.astype(jnp.bfloat16), 'mp').astype(jnp.float32)  30 us
    psum x1, blocking collectives, on_device(): squares = lax.psum(jnp.sum(stream * stream, axis=1), 'node')  21.4 us
    reduce_scatter x1, waiting for transfers between devices, on_device(): lax.psum_scatter(jnp.dot(act, down_weight, preferred_element_type=jnp.flo...  18.8 us
    dot_general x1, matrix products, on_device(): jnp.dot(act, down_weight, preferred_element_type=jnp.float32)  8.71 us
    dot_general x1, matrix products, on_device(): jnp.dot(normed, up_weight, preferred_element_type=jnp.float32)  8.67 us
  transfers between devices with their start and end apart: 6, of which 6 were waited for; matrix products, arithmetic and copies ran while one was open for 2% of the time, Pallas kernels for 0%

commit v1 on v0

--- a/solution.py
+++ b/solution.py
@@ -144,7 +144,9 @@
         out_weight,
         preferred_element_type=jnp.float32,
     )
-    projected = lax.psum(projected.astype(jnp.bfloat16), "mp").astype(jnp.float32)
+    projected = jnp.sum(
+        lax.all_gather(projected.astype(jnp.bfloat16), axis_name="mp"), axis=0
+    ).astype(jnp.float32)
     stream = residual.astype(jnp.float32) + projected
     squares = lax.psum(jnp.sum(stream * stream, axis=1), "node")
     normed = (stream * lax.rsqrt(squares[:, None] / D + norm_eps) * norm_gain[None, :]).astype(

time: 298 us -> 271 us (0.909)
  waiting for transfers between devices: 137 us -> 108 us
  blocking collectives: 84.5 us -> 87.6 us
    psum x1 -> x0, waiting for transfers between devices: 30 us -> none  [on_device(): lax.psum(projected.astype(jnp.bfloat16), 'mp').astype(jnp.float32)]
    all_gather x0 -> x1, blocking collectives: none -> 5.77 us  [on_device(): lax.all_gather(projected.astype(jnp.bfloat16), axis_name='mp')]
  transfers between devices with their start and end apart: 6 -> 5, of which waited for: 6 -> 5; matrix products, arithmetic and copies ran while one was open for 2% -> 2% of each run, Pallas kernels for 0% -> 0%
where the time goes in v1:
time: 271 us; the launch traced here: 270 us
  waiting for transfers between devices  108 us (40%)
  blocking collectives  87.6 us (32%)
  matrix products  37.3 us (14%)
  between operations  13.6 us (5%)
  starting transfers between devices  13 us (5%)
  local copies, waits for them, and re-layouts  5.72 us (2%)
  other arithmetic  4.53 us (2%)
    psum x1, waiting for transfers between devices, on_device(): lax.psum(jnp.dot(normed, up_weight, preferred_element_type=jnp.float32).a...  74.2 us
    all_gather x1, blocking collectives, on_device(): gathered = lax.all_gather(queries, 'node', axis=0, tiled=True)  32.5 us
    all_gather x1, blocking collectives, on_device(): lax.all_gather(attended, 'node', axis=0, tiled=True)  30.6 us
    reduce_scatter x1, waiting for transfers between devices, on_device(): lax.psum_scatter(jnp.dot(act, down_weight, preferred_element_type=jnp.flo...  18.8 us
    psum x1, blocking collectives, on_device(): squares = lax.psum(jnp.sum(stream * stream, axis=1), 'node')  18.8 us
    dot_general x1, matrix products, on_device(): jnp.dot(act, down_weight, preferred_element_type=jnp.float32)  8.71 us
    dot_general x1, matrix products, on_device(): jnp.dot(normed, gate_weight, preferred_element_type=jnp.float32)  8.62 us
    dot_general x1, matrix products, on_device(): jnp.dot(normed, up_weight, preferred_element_type=jnp.float32)  8.6 us
  transfers between devices with their start and end apart: 5, of which 5 were waited for; matrix products, arithmetic and copies ran while one was open for 2% of the time, Pallas kernels for 0%

profile of v1, /device:TPU:0, one launch (start us, length us, event | category | flops | bytes accessed | tf_op | source)
XLA Modules:
  0.0 270.1 jit_solution(3275656874343743828)
XLA Ops:
  6.5 0.0 copy-start
  6.5 1.3 dynamic_slice.18
  7.9 0.6 iota_compare_fusion.2
  8.5 0.7 compare_bitcast_fusion
  9.2 0.1 copy.97
  9.3 0.1 reduce-window.7
  9.3 0.1 add_reduce_fusion
  9.5 32.5 %all_gather.12 = bf16[32,16,128]{2,1,0:T(8,128)(2,1)S(1)} all-gather(bf16[4,16,128]{2,1,0:T(8,128)(2,1)} %param.16), channel_id=1, replica_groups=mesh['node'=8,'mp'=4] {'node'}, dimensions={0}, use_global_device_ids=true | all-gather | bytes 147456 | tf_op jit(solution)/shard_map/all_gather | solution.py:64
  42.1 0.1 convolution_convert_fusion.4
  42.2 1.4 fusion.79
  43.6 0.1 copy.100
  43.7 0.2 fusion.37
  43.9 0.1 copy.114
  44.0 0.0 copy-start.6
  44.0 2.1 bitcast_reduce_fusion
  46.1 0.0 copy-start.1
  46.1 0.1 subtract_exponential_fusion.1
  46.2 1.8 copy-done.1
  48.0 0.8 fusion.1
  48.9 0.0 copy-start.3
  48.9 0.1 fusion.22
  49.0 0.7 copy.115
  49.7 5.5 %all-to-all-start.2 = ((f32[32,2,8]{2,1,0:T(2,128)}), f32[32,2,8]{2,1,0:T(2,128)S(1)}, u32[]{:S(2)}, u32[]{:S(2)}) async-start(f32[32,2,8]{2,1,0:T(2,128)} %copy.115), calls=%async_computation.2 | async-start | bytes 65536 | tf_op jit(solution)/shard_map/all_to_all | solution.py:108
  55.1 0.0 copy-done.8
  55.1 0.1 iota_compare_fusion
  55.2 0.0 copy-done.6
  55.2 0.3 convolution_bitcast_fusion
  55.5 0.0 copy-done
  55.5 0.0 copy-start.7
  55.5 3.3 %fusion.13 = f32[32,2,8,128]{3,0,2,1:T(8,128)S(1)} fusion(f32[2,2048,32,8]{1,2,3,0:T(8,128)} %copy-done.1, f32[32,2,8]{0,2,1:T(8,128)S(1)} %get-tuple-element.48, bf16[2048,2,128,1]{2,1,0,3:T(2,128)(2,1)S(1)} %bitcast.76, f32[32,2,8]{0,2,1:T(8,128)S(1)} %subtract_exponential_fusion.2), kind=kOutput, calls=%fused_computation.16 | convolution fusion | flops 271646720 | bytes 5509120 | tf_op jit(solution)/shard_map/bkgl,lkd->bkgd/dot_general | solution.py:21
  58.8 0.0 copy-done.3
  58.8 0.0 copy-done.5
  58.8 0.3 fusion.80
  59.2 0.7 copy.104
  59.9 2.0 all-to-all-done.2
  61.8 4.0 %all-to-all-start.1 = ((f32[32,2,8]{2,1,0:T(2,128)}), f32[32,2,8]{2,1,0:T(2,128)S(1)}, u32[]{:S(2)}, u32[]{:S(2)}) async-start(f32[32,2,8]{2,1,0:T(2,128)} %copy.104), calls=%async_computation.1 | async-start | bytes 65536 | tf_op jit(solution)/shard_map/all_to_all | solution.py:107
  65.8 0.3 fusion.12
  66.2 0.0 copy-start.2
  66.2 0.0 copy-start.4
  66.2 0.8 copy.103
  67.0 5.5 %all-to-all-done.1 = f32[32,2,8]{2,1,0:T(2,128)S(1)} async-done(((f32[32,2,8]{2,1,0:T(2,128)}), f32[32,2,8]{2,1,0:T(2,128)S(1)}, u32[]{:S(2)}, u32[]{:S(2)}) %all-to-all-start.1) | async-done | bytes 2080 | tf_op jit(solution)/shard_map/all_to_all | solution.py:107
  72.5 3.4 %all-to-all-start = ((f32[32,2,8,128]{3,2,1,0:T(8,128)}), f32[32,2,8,128]{3,2,1,0:T(8,128)S(1)}, u32[]{:S(2)}, u32[]{:S(2)}) async-start(f32[32,2,8,128]{3,2,1,0:T(8,128)} %copy.103), calls=%async_computation | async-start | bytes 524288 | tf_op jit(solution)/shard_map/all_to_all | solution.py:109
  76.0 0.0 all-reduce.3.cloned.1.call-start
  76.0 0.2 fusion.45
  76.3 7.9 %all-to-all-done = f32[32,2,8,128]{3,2,1,0:T(8,128)S(1)} async-done(((f32[32,2,8,128]{3,2,1,0:T(8,128)}), f32[32,2,8,128]{3,2,1,0:T(8,128)S(1)}, u32[]{:S(2)}, u32[]{:S(2)}) %all-to-all-start) | async-done | bytes 262176 | tf_op jit(solution)/shard_map/all_to_all | solution.py:109
  84.2 0.1 fusion.40
  84.3 0.0 copy-done.7
  84.4 0.2 fusion.19
  84.6 30.6 %all-gather.1 = bf16[8,4,2048]{2,1,0:T(4,128)(2,1)S(1)} all-gather(bf16[1,4,2048]{2,1,0:T(4,128)(2,1)S(1)} %reshape.274), channel_id=1, replica_groups=mesh['node'=8,'mp'=4] {'node'}, dimensions={0}, use_global_device_ids=true | all-gather | bytes 147456 | tf_op jit(solution)/shard_map/all_gather | solution.py:143
  115.2 3.0 %convolution_convert_fusion.3 = bf16[32,1024]{1,0:T(8,128)(2,1)S(1)} fusion(bf16[32,2048]{1,0:T(8,128)(2,1)S(1)} %reshape.275, bf16[2048,1024]{1,0:T(8,128)(2,1)} %param.28), kind=kOutput, calls=%fused_computation.20 | convolution fusion | flops 134250496 | bytes 4390912 | tf_op jit(solution)/shard_map/dot_general | solution.py:142
  118.2 5.8 %all-gather = bf16[128,1024]{1,0:T(8,128)(2,1)S(1)} all-gather(bf16[32,1024]{1,0:T(8,128)(2,1)S(1)} %convolution_convert_fusion.3), channel_id=2, replica_groups=mesh['node'=8,'mp'=4] {'mp'}, dimensions={0}, use_global_device_ids=true | all-gather | bytes 327680 | tf_op jit(solution)/shard_map/all_gather | solution.py:148
  124.0 0.0 copy-done.2
  124.1 0.1 convert_add_fusion
  124.2 18.8 %psum.21 = f32[32]{0:T(128)S(1)} all-reduce(f32[32]{0:T(128)S(1)} %get-tuple-element.45), channel_id=1, replica_groups=mesh['node'=8,'mp'=4] {'node'}, use_global_device_ids=true, to_apply=%region_13.14 | all-reduce | flops 32 | bytes 256 | tf_op jit(solution)/shard_map/psum | solution.py:151
  143.0 0.0 copy-done.4
  143.0 8.6 %convolution_convert_fusion = bf16[32,7168]{1,0:T(8,128)(2,1)} fusion(bf16[1024,7168]{1,0:T(8,128)(2,1)} %param.30, f32[1024]{0:T(1024)S(1)} %copy-done.4, f32[32]{0:T(128)S(1)} %add_rsqrt_fusion, bf16[32,1024]{1,0:T(8,128)(2,1)S(1)} %reduce_sum.82, bf16[32,1024]{1,0:T(8,128)(2,1)S(1)} %copy-done.2), kind=kOutput, calls=%fused_computation | convolution fusion | flops 470188032 | bytes 15274112 | tf_op jit(solution)/shard_map/dot_general | solution.py:162
  151.6 8.6 %convolution_convert_fusion.1 = bf16[32,7168]{1,0:T(8,128)(2,1)} fusion(bf16[1024,7168]{1,0:T(8,128)(2,1)} %param.29, f32[1024]{0:T(1024)S(1)} %copy-done.4, f32[32]{0:T(128)S(1)} %add_rsqrt_fusion, bf16[32,1024]{1,0:T(8,128)(2,1)S(1)} %reduce_sum.82, bf16[32,1024]{1,0:T(8,128)(2,1)S(1)} %copy-done.2), kind=kOutput, calls=%fused_computation.1 | convolution fusion | flops 470188032 | bytes 15274112 | tf_op jit(solution)/shard_map/dot_general | solution.py:158
  160.2 0.0 all-reduce.3.cloned.1.call-update
  160.2 0.0 reduce-scatter.2.cloned.1.call-start
  160.3 74.2 %all-reduce.3.cloned.1.call-done = (bf16[32,7168]{1,0:T(8,128)(2,1)}, bf16[32,7168]{1,0:T(8,128)(2,1)}) async-done(((bf16[32,7168]{1,0:T(8,128)(2,1)}, bf16[32,7168]{1,0:T(8,128)(2,1)}), (bf16[32,7168]{1,0:T(8,128)(2,1)}, bf16[32,7168]{1,0:T(8,128)(2,1)})) %all-reduce.3.cloned.1.call-update) | async-done | bytes 917520 | tf_op jit(solution)/shard_map/psum | solution.py:161
  234.4 8.7 %convolution_convert_fusion.2 = bf16[32,1024]{1,0:T(8,128)(2,1)} fusion(bf16[7168,1024]{1,0:T(8,128)(2,1)} %param.31, bf16[32,7168]{1,0:T(8,128)(2,1)} %get-tuple-element.23, bf16[32,7168]{1,0:T(8,128)(2,1)} %get-tuple-element.24), kind=kOutput, calls=%fused_computation.19 | convolution fusion | flops 471629824 | bytes 15663104 | tf_op jit(solution)/shard_map/dot_general | solution.py:168
  243.1 0.0 reduce-scatter.2.cloned.1.call-update
  243.2 18.8 %reduce-scatter.2.cloned.1.call-done = bf16[8,1024]{1,0:T(8,128)(2,1)} async-done(((bf16[32,1024]{1,0:T(8,128)(2,1)}), bf16[8,1024]{1,0:T(8,128)(2,1)}) %reduce-scatter.2.cloned.1.call-update) | async-done | bytes 16400 | tf_op jit(solution)/shard_map/reduce_scatter | solution.py:167
  262.0 1.3 add_convert_fusion
  (18 shorter events, 0.3 us)
Async XLA Ops:
  6.5 49.0 %copy-start = (bf16[2048,2,128]{2,1,0:T(2,128)(2,1)S(1)}, bf16[2048,2,128]{2,1,0:T(2,128)(2,1)}, u32[]{:S(2)}) copy-start(bf16[2048,2,128]{2,1,0:T(2,128)(2,1)} %param.18) | copy-start | bytes 3145732
  44.0 11.1 %copy-start.8 = (s32[4]{0:T(128)S(1)}, s32[4]{0:T(128)}, u32[]{:S(2)}) copy-start(s32[4]{0:T(128)} %param.24) | copy-start | bytes 52
  44.0 11.2 %copy-start.6 = (bf16[1,1024,2,128]{3,2,1,0:T(2,128)(2,1)S(1)}, bf16[1,1024,2,128]{3,2,1,0:T(2,128)(2,1)}, u32[]{:S(2)}) copy-start(bf16[1,1024,2,128]{3,2,1,0:T(2,128)(2,1)} %param.20) | copy-start | bytes 1572868
  46.1 1.9 copy-start.1
  48.9 10.0 %copy-start.3 = (bf16[4,256,2,128]{3,2,1,0:T(2,128)(2,1)S(1)}, bf16[4,256,2,128]{3,2,1,0:T(2,128)(2,1)}, u32[]{:S(2)}) copy-start(bf16[4,256,2,128]{3,2,1,0:T(2,128)(2,1)} %param.21) | copy-start | bytes 1572868
  48.9 10.0 %copy-start.5 = (bf16[4,16,128]{2,1,0:T(8,128)(2,1)S(1)}, bf16[4,16,128]{2,1,0:T(8,128)(2,1)}, u32[]{:S(2)}) copy-start(bf16[4,16,128]{2,1,0:T(8,128)(2,1)} %param.16) | copy-start | bytes 49156
  49.7 12.1 %all-to-all-start.2 = ((f32[32,2,8]{2,1,0:T(2,128)}), f32[32,2,8]{2,1,0:T(2,128)S(1)}, u32[]{:S(2)}, u32[]{:S(2)}) async-start(f32[32,2,8]{2,1,0:T(2,128)} %copy.115), calls=%async_computation.2 | async-start | bytes 65536 | tf_op jit(solution)/shard_map/all_to_all | solution.py:108
  55.5 28.8 %copy-start.7 = (bf16[4,256,2,128]{3,2,1,0:T(2,128)(2,1)S(1)}, bf16[4,256,2,128]{3,2,1,0:T(2,128)(2,1)}, u32[]{:S(2)}) copy-start(bf16[4,256,2,128]{3,2,1,0:T(2,128)(2,1)} %param.22) | copy-start | bytes 1572868
  61.8 10.7 %all-to-all-start.1 = ((f32[32,2,8]{2,1,0:T(2,128)}), f32[32,2,8]{2,1,0:T(2,128)S(1)}, u32[]{:S(2)}, u32[]{:S(2)}) async-start(f32[32,2,8]{2,1,0:T(2,128)} %copy.104), calls=%async_computation.1 | async-start | bytes 65536 | tf_op jit(solution)/shard_map/all_to_all | solution.py:107
  66.2 57.9 %copy-start.2 = (bf16[32,1024]{1,0:T(8,128)(2,1)S(1)}, bf16[32,1024]{1,0:T(8,128)(2,1)}, u32[]{:S(2)}) copy-start(bf16[32,1024]{1,0:T(8,128)(2,1)} %param.26) | copy-start | bytes 196612
  66.2 76.8 %copy-start.4 = (f32[1024]{0:T(1024)S(1)}, f32[1024]{0:T(1024)}, u32[]{:S(2)}) copy-start(f32[1024]{0:T(1024)} %param.27) | copy-start | bytes 12292
  72.5 11.7 %all-to-all-start = ((f32[32,2,8,128]{3,2,1,0:T(8,128)}), f32[32,2,8,128]{3,2,1,0:T(8,128)S(1)}, u32[]{:S(2)}, u32[]{:S(2)}) async-start(f32[32,2,8,128]{3,2,1,0:T(8,128)} %copy.103), calls=%async_computation | async-start | bytes 524288 | tf_op jit(solution)/shard_map/all_to_all | solution.py:109
  76.0 158.5 %all-reduce.3.cloned.1.call-start = ((), (), s32[]{:S(2)}) async-start(), calls=%async_computation.5 | async-start | bytes 1835008 | tf_op jit(solution)/shard_map/psum | solution.py:161
  160.2 101.8 %reduce-scatter.2.cloned.1.call-start = ((), (), s32[]{:S(2)}) async-start(), calls=%async_computation.4 | async-start | bytes 81920 | tf_op jit(solution)/shard_map/reduce_scatter | solution.py:167
Sparse Core Ops, SparseCore 0:
  160.3 74.0 all-reduce.2
  243.3 18.6 reduce-scatter.1
